TPU v7x, 128 devices: a whole 4x4x4 slice. The times are simulated.
128 devices in a mesh: row: 16 (over y, x), col: 8 (over z, core).
Axes of the slice: x: 4, y: 4, z: 4, core: 2. Of those that a mesh axis runs over, the one named last changes fastest.
Arguments:
- row_emb: float32 [128, 300, 1024], P(('row', 'col')), may hold values from -1.5 to 1.5
- col_emb: float32 [128, 300, 1024], P(('row', 'col')), may hold values from -1.5 to 1.5
- row_acc: float32 [128, 300, 1024], P(('row', 'col')), may hold values from 0.5 to 8
- col_acc: float32 [128, 300, 1024], P(('row', 'col')), may hold values from 0.5 to 8
- marginal_log: float32 [131072], replicated, may hold values from -2 to 1
- tile_rows: int32 [384], P(('row', 'col')), may hold values from 0 to 127, as said below
- tile_cols: int32 [384], P(('row', 'col')), may hold values from 0 to 127, as said below
- counts: int32 [384, 1024, 1024], P(('row', 'col')), may hold values from 0 to 2047
Outputs:
- new_row_emb: float32 [128, 300, 1024], P(('row', 'col'))
- new_col_emb: float32 [128, 300, 1024], P(('row', 'col'))
- new_row_acc: float32 [128, 300, 1024], P(('row', 'col'))
- new_col_acc: float32 [128, 300, 1024], P(('row', 'col'))
Inputs may be any that keep to these rules, and one draw needn't show every extreme that they name: Block g of the embeddings lies on device g in the mesh's order (row slowest). Slot k lies on device p = k // 3; with p at row index r and col index c, tile_rows[k] // 8 equals r. With slot k on the device at col index c, tile_cols[k] % 8 equals c.
All inputs are finite; a program needn't handle non-finite values.
Results may differ from a plain program's by a relative error of at most 0.019.
Values may be sent and summed in bfloat16 or wider, within the bound.
No kernel may reach another device: no remote copies, remote signals or barrier semaphores. Data moves between devices by JAX's collectives and lax.ppermute only.
A program may use at most 128 MiB of HBM per device.

v0:
```python
import jax
import jax.numpy as jnp
from jax import lax
from jax.sharding import PartitionSpec as P

err_scale = 0.03125
learn_rate = 0.1


def split_up(array, dim, length):
    before, after = (array.shape[:dim], array.shape[dim + 1 :])
    return jnp.moveaxis(array.reshape(*before, length, -1, *after), dim, 0)


def sum_at_owner(array, axis, dim):
    length = lax.axis_size(axis)
    pieces = lax.all_to_all(split_up(array, dim, length), axis, 0, 0, tiled=True)
    return jnp.sum(pieces.astype(jnp.float32), axis=0)


def tile_terms(row_block, col_block, tile_counts, row_margin, col_margin):
    scores = lax.dot_general(
        row_block, col_block, (((0,), (0,)), ((), ())), preferred_element_type=jnp.float32
    )
    counted = tile_counts.astype(jnp.float32)
    shifted_log = jnp.log(jnp.maximum(counted, 1.0)) - row_margin[:, None] - col_margin[None, :]
    residue = scores - shifted_log
    weighted = (0.1 + 0.25 * jnp.sqrt(counted)) * residue
    cell_grad = jnp.where(tile_counts > 0, weighted, jax.nn.sigmoid(residue)) * err_scale
    errors = cell_grad.astype(jnp.bfloat16)
    row_term = lax.dot_general(
        col_block, errors, (((1,), (1,)), ((), ())), preferred_element_type=jnp.float32
    )
    col_term = jnp.dot(row_block, errors, preferred_element_type=jnp.float32)
    return (row_term, col_term)


def add_slot(buffer, slot_index, term):
    old_value = lax.dynamic_index_in_dim(buffer, slot_index, 0, keepdims=False)
    return lax.dynamic_update_index_in_dim(buffer, old_value + term, slot_index, 0)


def adagrad(weights, history, gradient):
    grown = history + gradient * gradient
    return (weights - learn_rate * gradient / jnp.sqrt(grown), grown)


def body(row_emb, col_emb, row_acc, col_acc, marginal_log, tile_rows, tile_cols, counts):
    col_count = lax.axis_size("col")
    row_count = lax.axis_size("row")
    emb_width = row_emb.shape[1]
    block_len = row_emb.shape[2]
    tile_total = counts.shape[0]
    row_low = row_emb.astype(jnp.bfloat16)
    col_low = col_emb.astype(jnp.bfloat16)
    rows_near = lax.all_gather(row_low, "col", axis=0, tiled=True)
    grads = (
        jnp.zeros((col_count, emb_width, block_len), jnp.float32),
        jnp.zeros((row_count, emb_width, block_len), jnp.float32),
    )
    cols_near = lax.all_gather(col_low, "row", axis=0, tiled=True)
    for tile_slot in range(tile_total):
        col_slot = tile_cols[tile_slot] // col_count
        col_block = lax.dynamic_index_in_dim(cols_near, col_slot, 0, keepdims=False)
        row_id = tile_rows[tile_slot]
        col_id = tile_cols[tile_slot]
        row_slot = row_id % col_count
        apply_col_slot = col_id // col_count
        row_block = lax.dynamic_index_in_dim(rows_near, row_slot, 0, keepdims=False)
        row_margin = lax.dynamic_slice_in_dim(marginal_log, row_id * block_len, block_len)
        col_margin = lax.dynamic_slice_in_dim(marginal_log, col_id * block_len, block_len)
        row_term, col_term = tile_terms(
            row_block, col_block, counts[tile_slot], row_margin, col_margin
        )
        grads = (
            add_slot(grads[0], row_slot, row_term),
            add_slot(grads[1], apply_col_slot, col_term),
        )
    row_sum = sum_at_owner(grads[0].astype(jnp.bfloat16), "col", 0)
    col_sum = lax.psum_scatter(
        grads[1].astype(jnp.bfloat16), "row", scatter_dimension=0, tiled=True
    ).astype(jnp.float32)
    new_row_emb, new_row_acc = adagrad(row_emb, row_acc, row_sum)
    new_col_emb, new_col_acc = adagrad(col_emb, col_acc, col_sum)
    return (new_row_emb, new_col_emb, new_row_acc, new_col_acc)


def solution(mesh):
    placed = (
        P(("row", "col"), None, None),
        P(("row", "col"), None, None),
        P(("row", "col"), None, None),
        P(("row", "col"), None, None),
        P(),
        P(("row", "col")),
        P(("row", "col")),
        P(("row", "col"), None, None),
    )
    return jax.shard_map(
        body,
        mesh=mesh,
        in_specs=placed,
        out_specs=(
            P(("row", "col"), None, None),
            P(("row", "col"), None, None),
            P(("row", "col"), None, None),
            P(("row", "col"), None, None),
        ),
        check_vma=False,
    )
```

profile of v0, /device:TPU:0, one launch (start us, length us, event | category | flops | bytes accessed | tf_op | source)
XLA Modules:
  0.0 274.2 jit_solution(9816080059861527763)
XLA Ops:
  7.2 2.3 copy.28
  9.6 2.3 copy.29
  12.0 0.6 fusion.64
  20.0 0.6 fusion.63
  30.0 0.8 fusion.62
  30.8 17.6 %all-gather.5.cloned.1.call-done = bf16[8,300,1024]{2,1,0:T(8,128)(2,1)} async-done(((bf16[1,300,1024]{2,1,0:T(8,128)(2,1)}), bf16[8,300,1024]{2,1,0:T(8,128)(2,1)}) %all-gather.5.cloned.1.call-update) | async-done | bytes 4915216 | tf_op jit(solution)/shard_map/all_gather | solution.py:56
  48.3 80.5 %all-gather.3.cloned.1.call-done = bf16[16,300,1024]{2,1,0:T(8,128)(2,1)} async-done(((bf16[1,300,1024]{2,1,0:T(8,128)(2,1)}), bf16[16,300,1024]{2,1,0:T(8,128)(2,1)}) %all-gather.3.cloned.1.call-update) | async-done | bytes 9830416 | tf_op jit(solution)/shard_map/all_gather | solution.py:61
  128.8 8.2 %fusion.14 = bf16[1024,1024]{1,0:T(8,128)(2,1)} fusion(s32[3,1024,1024]{2,1,0:T(8,128)} %param.15, f32[1024]{0:T(1024)S(1)} %get-tuple-element.17, f32[1024]{0:T(1024)S(1)} %get-tuple-element.18, bf16[8,300,1024]{2,1,0:T(8,128)(2,1)} %all-gather.5.cloned.1.call-done, s32[]{:T(128)S(6)} %select_n.95, ...), kind=kOutput, calls=%fused_computation.22 | convolution fusion | flops 644874240 | bytes 7544840 | tf_op jit(solution)/shard_map/dot_general | solution.py:22
  137.0 9.2 %broadcast_in_dim.36 = f32[16,300,1024]{2,1,0:T(8,128)} broadcast(f32[]{:T(128)} %constant.108.clone.1), dimensions={} | broadcast | bytes 19660804 | tf_op jit(solution)/shard_map/broadcast_in_dim | solution.py:59
  146.2 3.0 %fusion.23 = f32[16,300,1024]{2,1,0:T(8,128)} fusion(f32[16,300,1024]{2,1,0:T(8,128)} %broadcast_in_dim.36, s32[]{:T(128)S(6)} %select_n.93, bf16[1024,1024]{1,0:T(8,128)(2,1)S(1)} %copy-done.8, bf16[8,300,1024]{2,1,0:T(8,128)(2,1)} %all-gather.5.cloned.1.call-done, s32[]{:T(128)S(6)} %select_n.95), kind=kOutput, calls=%fused_computation.38 | convolution fusion | flops 629145600 | bytes 3964936 | tf_op jit(solution)/shard_map/dot_general | solution.py:34
  149.2 1.5 constant_dynamic-slice_fusion.3
  150.8 5.6 %fusion.9 = bf16[1024,1024]{1,0:T(8,128)(2,1)S(1)} fusion(s32[3,1024,1024]{2,1,0:T(8,128)S(1)} %bitcast.136, f32[1024]{0:T(1024)S(1)} %get-tuple-element.15, f32[1024]{0:T(1024)S(1)} %get-tuple-element.16, bf16[8,300,1024]{2,1,0:T(8,128)(2,1)} %all-gather.5.cloned.1.call-done, s32[]{:T(128)S(6)} %select_n.100, ...), kind=kOutput, calls=%fused_computation.15 | convolution fusion | flops 644874240 | bytes 7544840 | tf_op jit(solution)/shard_map/dot_general | solution.py:22
  156.4 0.5 slice-done.4
  156.9 1.9 fusion.18
  159.0 5.6 %fusion.4 = bf16[1024,1024]{1,0:T(8,128)(2,1)S(1)} fusion(s32[3,1024,1024]{2,1,0:T(8,128)S(1)} %bitcast.136, f32[1024]{0:T(1024)S(1)} %get-tuple-element.19, f32[1024]{0:T(1024)S(1)} %get-tuple-element.14, bf16[8,300,1024]{2,1,0:T(8,128)(2,1)} %all-gather.5.cloned.1.call-done, s32[]{:T(128)S(6)} %select_n.107, ...), kind=kOutput, calls=%fused_computation.8 | convolution fusion | flops 644874240 | bytes 7544840 | tf_op jit(solution)/shard_map/dot_general | solution.py:22
  164.6 1.3 copy-done.2
  165.9 1.9 fusion.16
  167.8 5.0 %convert_element_type.49 = bf16[16,300,1024]{2,1,0:T(8,128)(2,1)} convert(f32[16,300,1024]{2,1,0:T(8,128)S(1)} %fusion.16) | non-fusion elementwise | flops 4915200 | bytes 29491200 | tf_op jit(solution)/shard_map/convert_element_type | solution.py:81
  172.8 1.3 broadcast_in_dim.32
  174.4 1.9 fusion.24
  176.4 2.1 fusion.22
  178.6 1.9 fusion.20
  180.6 0.8 convert_bitcast_fusion
  181.4 62.3 %all_to_all.5 = bf16[8,1,300,1024]{3,2,1,0:T(8,128)(2,1)S(1)} all-to-all(bf16[8,1,300,1024]{3,2,1,0:T(8,128)(2,1)S(1)} %convert_bitcast_fusion), channel_id=1, replica_groups=mesh['row'=16,'col'=8] {'col'}, dimensions={0} | all-to-all | bytes 9830400 | tf_op jit(solution)/shard_map/all_to_all | solution.py:17
  243.7 1.1 convert_reduce_fusion
  244.9 0.4 multiply_bitcast_fusion
  245.2 0.5 copy-done.4
  245.8 5.8 %multiply_subtract_fusion = (f32[1,300,1024]{2,0,1:T(1,128)}, f32[1,300,1024]{2,0,1:T(1,128)}) fusion(f32[1,300,1024]{2,0,1:T(1,128)S(1)} %copy-done, f32[300,1024]{1,0:T(8,128)S(1)} %get-tuple-element.13, f32[1,300,1024]{2,0,1:T(1,128)S(1)} %copy-done.4, f32[1,300,1024]{2,1,0:T(8,128)S(1)} %get-tuple-element.12), kind=kLoop, calls=%fused_computation.47 | loop fusion | flops 921600 | bytes 7372800 | tf_op jit(solution)/shard_map/sub | solution.py:45
  251.6 9.8 %reduce-scatter.4.cloned.1.call-done = bf16[1,300,1024]{2,1,0:T(8,128)(2,1)} async-done(((bf16[16,300,1024]{2,1,0:T(8,128)(2,1)}), bf16[1,300,1024]{2,1,0:T(8,128)(2,1)}) %reduce-scatter.4.cloned.1.call-update) | async-done | bytes 614416
  261.4 1.8 fusion.26
  263.1 2.3 copy.21
  265.4 2.3 copy.22
  (44 shorter events, 0.9 us)
Async XLA Ops:
  7.2 4.8 %copy-start.6 = (s32[3]{0:T(128)S(1)}, s32[3]{0:T(128)}, u32[]{:S(2)}) copy-start(s32[3]{0:T(128)} %param.13) | copy-start | bytes 40
  7.2 12.9 %copy-start.7 = (s32[3]{0:T(128)S(1)}, s32[3]{0:T(128)}, u32[]{:S(2)}) copy-start(s32[3]{0:T(128)} %param.14) | copy-start | bytes 40
  7.2 41.2 %all-gather.5.cloned.1.call-start = ((), (), s32[]{:S(2)}) async-start(), calls=%async_computation.3 | async-start | bytes 5603328 | tf_op jit(solution)/shard_map/all_gather | solution.py:56
  9.6 119.3 %all-gather.3.cloned.1.call-start = ((), (), s32[]{:S(2)}) async-start(), calls=%async_computation.2 | async-start | bytes 10584064 | tf_op jit(solution)/shard_map/all_gather | solution.py:61
  11.9 249.4 %reduce-scatter.4.cloned.1.call-start = ((), (), s32[]{:S(2)}) async-start(), calls=%async_computation.4 | async-start | bytes 10584064
  128.8 21.9 %slice-start.5 = ((s8[12582912]{0:T(1024)(128)(4,1)}), s8[4194304]{0:T(1024)(128)(4,1)S(1)}, s32[]{:S(2)}) async-start(s8[12582912]{0:T(1024)(128)(4,1)} %bitcast.135), calls=%async_computation.10 | async-start | bytes 8388608
  128.8 21.9 %slice-start.6 = ((s8[12582912]{0:T(1024)(128)(4,1)}), s8[4194304]{0:T(1024)(128)(4,1)S(1)}, s32[]{:S(2)}) async-start(s8[12582912]{0:T(1024)(128)(4,1)} %bitcast.135), calls=%async_computation.11 | async-start | bytes 8388608
  137.0 9.3 %copy-start.8 = (bf16[1024,1024]{1,0:T(8,128)(2,1)S(1)}, bf16[1024,1024]{1,0:T(8,128)(2,1)}, u32[]{:S(2)}) copy-start(bf16[1024,1024]{1,0:T(8,128)(2,1)} %fusion.14) | copy-start | bytes 6291460
  137.0 13.8 %slice-start.7 = ((s8[12582912]{0:T(1024)(128)(4,1)}), s8[4194304]{0:T(1024)(128)(4,1)S(1)}, s32[]{:S(2)}) async-start(s8[12582912]{0:T(1024)(128)(4,1)} %bitcast.135), calls=%async_computation.12 | async-start | bytes 8388608
  149.2 7.2 %slice-start = ((s8[19922944]{0:T(1024)(128)(4,1)}), s8[4194304]{0:T(1024)(128)(4,1)S(1)}, s32[]{:S(2)}) async-start(s8[19922944]{0:T(1024)(128)(4,1)} %bitcast.133), calls=%async_computation.5 | async-start | bytes 8388608
  150.8 5.6 %slice-start.1 = ((s8[19922944]{0:T(1024)(128)(4,1)}), s8[4194304]{0:T(1024)(128)(4,1)S(1)}, s32[]{:S(2)}) async-start(s8[19922944]{0:T(1024)(128)(4,1)} %bitcast.133), calls=%async_computation.6 | async-start | bytes 8388608
  150.8 5.6 %slice-start.2 = ((s8[19922944]{0:T(1024)(128)(4,1)}), s8[4194304]{0:T(1024)(128)(4,1)S(1)}, s32[]{:S(2)}) async-start(s8[19922944]{0:T(1024)(128)(4,1)} %bitcast.133), calls=%async_computation.7 | async-start | bytes 8388608
  150.8 5.6 %slice-start.3 = ((s8[19922944]{0:T(1024)(128)(4,1)}), s8[4194304]{0:T(1024)(128)(4,1)S(1)}, s32[]{:S(2)}) async-start(s8[19922944]{0:T(1024)(128)(4,1)} %bitcast.133), calls=%async_computation.8 | async-start | bytes 8388608
  150.8 6.1 %slice-start.4 = ((s8[19922944]{0:T(1024)(128)(4,1)}), s8[3145728]{0:T(1024)(128)(4,1)S(1)}, s32[]{:S(2)}) async-start(s8[19922944]{0:T(1024)(128)(4,1)} %bitcast.133), calls=%async_computation.9 | async-start | bytes 6291456
  164.6 1.3 copy-start.2
  172.8 1.6 copy-start.9
  176.4 2.2 copy-start.3
  243.7 1.5 copy-start
  243.7 2.1 copy-start.4
  245.2 16.2 %copy-start.1 = (f32[1,300,1024]{2,0,1:T(1,128)S(1)}, f32[1,300,1024]{2,0,1:T(1,128)}, u32[]{:S(2)}) copy-start(f32[1,300,1024]{2,0,1:T(1,128)} %param.9) | copy-start | bytes 3686404
  245.2 16.1 %copy-start.5 = (f32[1,300,1024]{2,0,1:T(1,128)S(1)}, f32[1,300,1024]{2,0,1:T(1,128)}, u32[]{:S(2)}) copy-start(f32[1,300,1024]{2,0,1:T(1,128)} %param.11) | copy-start | bytes 3686404
Sparse Core Ops, SparseCore 0:
  10.3 38.0 all-gather.4
  51.0 77.7 all-gather.2
  172.9 88.4 reduce-scatter.3
where the time goes:
time: 275 us; the launch traced here: 274 us
  waiting for transfers between devices  108 us (39%)
  blocking collectives  62.3 us (23%)
  matrix products  32 us (12%)
  between operations  30.9 us (11%)
  local copies, waits for them, and re-layouts  26.2 us (10%)
  other arithmetic  14.8 us (5%)
    all_gather x1, waiting for transfers between devices, body(): cols_near = lax.all_gather(col_low, 'row', axis=0, tiled=True)  80.5 us
    all_to_all x1, blocking collectives, sum_at_owner(): lax.all_to_all(split_up(array, dim, length), axis, 0, 0, tiled=True)  62.3 us
    dot_general x3, matrix products, tile_terms(): lax.dot_general(row_block, col_block, (((0,), (0,)), ((), ())), preferred...  19.3 us
    all_gather x1, waiting for transfers between devices, body(): rows_near = lax.all_gather(row_low, 'col', axis=0, tiled=True)  17.6 us
    unnamed x40, local copies, waits for them, and re-layouts  11.9 us
    unnamed x4, waiting for transfers between devices  9.82 us
    broadcast_in_dim x1, local copies, waits for them, and re-layouts, body(): jnp.zeros((row_count, emb_width, block_len), jnp.float32)  9.25 us
    sub x2, other arithmetic, adagrad(): return (weights - learn_rate * gradient / jnp.sqrt(grown), grown)  7.58 us
  transfers between devices with their start and end apart: 3, of which 3 were waited for; matrix products, arithmetic and copies ran while one was open for 7% of the time, Pallas kernels for 0%

commit v1 on v0

--- a/solution.py
+++ b/solution.py
@@ -58,7 +58,9 @@
         jnp.zeros((col_count, emb_width, block_len), jnp.float32),
         jnp.zeros((row_count, emb_width, block_len), jnp.float32),
     )
-    cols_near = lax.all_gather(col_low, "row", axis=0, tiled=True)
+    cols_near = jnp.concatenate(
+        lax.all_to_all(jnp.stack([col_low] * lax.axis_size("row")), "row", 0, 0), axis=0
+    )
     for tile_slot in range(tile_total):
         col_slot = tile_cols[tile_slot] // col_count
         col_block = lax.dynamic_index_in_dim(cols_near, col_slot, 0, keepdims=False)

time: 275 us -> 318 us (1.16)
  waiting for transfers between devices: 108 us -> 137 us
  starting transfers between devices: 0.12 us -> 7.59 us
    all_to_all x0 -> x1, waiting for transfers between devices: none -> 107 us  [body(): lax.all_to_all(jnp.stack([col_low] * lax.axis_size('row')), 'row', 0, 0)]
    all_gather x1 -> x0, waiting for transfers between devices: 80.5 us -> none  [body(): cols_near = lax.all_gather(col_low, 'row', axis=0, tiled=True)]
    all_to_all x0 -> x1, starting transfers between devices: none -> 7.32 us  [body(): lax.all_to_all(jnp.stack([col_low] * lax.axis_size('row')), 'row', 0, 0)]
    another operation x0 -> x1, local copies, waits for them, and re-layouts: none -> 5.1 us  [body(): jnp.stack([col_low] * lax.axis_size('row'))]
    unnamed x40 -> x38, local copies, waits for them, and re-layouts: 11.9 us -> 7.98 us
    unnamed x4 -> x3, waiting for transfers between devices: 9.82 us -> 10.4 us
  transfers between devices with their start and end apart: 3 -> 3, of which waited for: 3 -> 3; matrix products, arithmetic and copies ran while one was open for 7% -> 6% of each run, Pallas kernels for 0% -> 0%
where the time goes in v1:
time: 318 us; the launch traced here: 317 us
  waiting for transfers between devices  137 us (43%)
  blocking collectives  63.2 us (20%)
  matrix products  32.1 us (10%)
  between operations  32 us (10%)
  local copies, waits for them, and re-layouts  27.4 us (9%)
  other arithmetic  17.5 us (6%)
  starting transfers between devices  7.59 us (2%)
    all_to_all x1, waiting for transfers between devices, body(): lax.all_to_all(jnp.stack([col_low] * lax.axis_size('row')), 'row', 0, 0)  107 us
    all_to_all x1, blocking collectives, sum_at_owner(): lax.all_to_all(split_up(array, dim, length), axis, 0, 0, tiled=True)  63.2 us
    all_gather x1, waiting for transfers between devices, body(): rows_near = lax.all_gather(row_low, 'col', axis=0, tiled=True)  20.2 us
    dot_general x3, matrix products, tile_terms(): lax.dot_general(row_block, col_block, (((0,), (0,)), ((), ())), preferred...  19.4 us
    unnamed x3, waiting for transfers between devices  10.4 us
    broadcast_in_dim x1, local copies, waits for them, and re-layouts, body(): jnp.zeros((row_count, emb_width, block_len), jnp.float32)  9.26 us
    sub x2, other arithmetic, adagrad(): return (weights - learn_rate * gradient / jnp.sqrt(grown), grown)  8.14 us
    unnamed x38, local copies, waits for them, and re-layouts  7.98 us
  transfers between devices with their start and end apart: 3, of which 3 were waited for; matrix products, arithmetic and copies ran while one was open for 6% of the time, Pallas kernels for 0%

profile of v1, /device:TPU:0, one launch (start us, length us, event | category | flops | bytes accessed | tf_op | source)
XLA Modules:
  0.0 317.0 jit_solution(14954891264257005293)
XLA Ops:
  7.2 2.1 convert_element_type.41
  9.5 5.1 %stack.2 = bf16[16,1,300,1024]{3,2,1,0:T(8,128)(2,1)} broadcast(bf16[300,1024]{1,0:T(8,128)(2,1)S(1)} %bitcast.138), dimensions={2,3} | broadcast | bytes 10444800 | tf_op jit(solution)/shard_map/stack | solution.py:62
  14.6 7.3 %all-to-all-start = ((bf16[16,1,300,1024]{3,2,1,0:T(8,128)(2,1)}), bf16[16,1,300,1024]{3,2,1,0:T(8,128)(2,1)}, u32[]{:S(2)}, u32[]{:S(2)}) async-start(bf16[16,1,300,1024]{3,2,1,0:T(8,128)(2,1)} %stack.2), calls=%async_computation | async-start | bytes 19922944 | tf_op jit(solution)/shard_map/all_to_all | solution.py:62
  22.0 1.0 copy.28
  23.3 0.6 fusion.64
  31.7 0.6 fusion.63
  42.1 0.8 fusion.62
  42.9 20.2 %all-gather.2.cloned.1.call-done = bf16[8,300,1024]{2,1,0:T(8,128)(2,1)} async-done(((bf16[1,300,1024]{2,1,0:T(8,128)(2,1)}), bf16[8,300,1024]{2,1,0:T(8,128)(2,1)}) %all-gather.2.cloned.1.call-update) | async-done | bytes 4915216 | tf_op jit(solution)/shard_map/all_gather | solution.py:56
  63.1 106.6 %all-to-all-done = bf16[16,1,300,1024]{3,2,1,0:T(8,128)(2,1)} async-done(((bf16[16,1,300,1024]{3,2,1,0:T(8,128)(2,1)}), bf16[16,1,300,1024]{3,2,1,0:T(8,128)(2,1)}, u32[]{:S(2)}, u32[]{:S(2)}) %all-to-all-start) | async-done | bytes 9830432 | tf_op jit(solution)/shard_map/all_to_all | solution.py:62
  169.7 8.2 %fusion.14 = bf16[1024,1024]{1,0:T(8,128)(2,1)} fusion(s32[3,1024,1024]{2,1,0:T(8,128)} %param.15, f32[1024]{0:T(1024)S(1)} %get-tuple-element.17, f32[1024]{0:T(1024)S(1)} %get-tuple-element.18, bf16[8,300,1024]{2,1,0:T(8,128)(2,1)} %all-gather.2.cloned.1.call-done, s32[]{:T(128)S(6)} %select_n.95, bf16[16,1,300,1024]{3,2,1,0:T(8,128)(2,1)} %all-to-all-done, ...), kind=kOutput, calls=%fused_computation.22 | convolution fusion | flops 644874240 | bytes 7544840 | tf_op jit(solution)/shard_map/dot_general | solution.py:22
  177.9 9.3 %broadcast_in_dim.36 = f32[16,300,1024]{2,1,0:T(8,128)} broadcast(f32[]{:T(128)} %constant.111.clone.1), dimensions={} | broadcast | bytes 19660804 | tf_op jit(solution)/shard_map/broadcast_in_dim | solution.py:59
  187.1 3.0 fusion.23
  190.1 1.5 constant_dynamic-slice_fusion.3
  191.7 5.6 %fusion.9 = bf16[1024,1024]{1,0:T(8,128)(2,1)S(1)} fusion(s32[3,1024,1024]{2,1,0:T(8,128)S(1)} %bitcast.140, f32[1024]{0:T(1024)S(1)} %get-tuple-element.15, f32[1024]{0:T(1024)S(1)} %get-tuple-element.16, bf16[8,300,1024]{2,1,0:T(8,128)(2,1)} %all-gather.2.cloned.1.call-done, s32[]{:T(128)S(6)} %select_n.100, bf16[16,1,300,1024]{3,2,1,0:T(8,128)(2,1)} %all-to-all-done, ...), kind=kOutput, calls=%fused_computation.15 | convolution fusion | flops 644874240 | bytes 7544840 | tf_op jit(solution)/shard_map/dot_general | solution.py:22
  197.3 0.5 slice-done.4
  197.8 1.9 fusion.18
  199.9 5.6 %fusion.4 = bf16[1024,1024]{1,0:T(8,128)(2,1)S(1)} fusion(s32[3,1024,1024]{2,1,0:T(8,128)S(1)} %bitcast.140, f32[1024]{0:T(1024)S(1)} %get-tuple-element.19, f32[1024]{0:T(1024)S(1)} %get-tuple-element.14, bf16[8,300,1024]{2,1,0:T(8,128)(2,1)} %all-gather.2.cloned.1.call-done, s32[]{:T(128)S(6)} %select_n.107, bf16[16,1,300,1024]{3,2,1,0:T(8,128)(2,1)} %all-to-all-done, ...), kind=kOutput, calls=%fused_computation.8 | convolution fusion | flops 644874240 | bytes 7544840 | tf_op jit(solution)/shard_map/dot_general | solution.py:22
  205.5 1.3 copy-done.2
  206.8 1.9 fusion.16
  208.7 5.0 %convert_element_type.52 = bf16[16,300,1024]{2,1,0:T(8,128)(2,1)} convert(f32[16,300,1024]{2,1,0:T(8,128)S(1)} %fusion.16) | non-fusion elementwise | flops 4915200 | bytes 29491200 | tf_op jit(solution)/shard_map/convert_element_type | solution.py:83
  213.8 1.3 broadcast_in_dim.32
  215.3 1.9 fusion.24
  217.4 2.1 fusion.22
  219.6 1.9 fusion.20
  221.5 0.8 convert_bitcast_fusion
  222.3 63.2 %all_to_all.10 = bf16[8,1,300,1024]{3,2,1,0:T(8,128)(2,1)S(1)} all-to-all(bf16[8,1,300,1024]{3,2,1,0:T(8,128)(2,1)S(1)} %convert_bitcast_fusion), channel_id=1, replica_groups=mesh['row'=16,'col'=8] {'col'}, dimensions={0} | all-to-all | bytes 9830400 | tf_op jit(solution)/shard_map/all_to_all | solution.py:17
  285.5 1.1 convert_reduce_fusion
  287.0 6.0 %multiply_subtract_fusion = (f32[1,300,1024]{2,0,1:T(1,128)}, f32[1,300,1024]{2,0,1:T(1,128)}) fusion(f32[1,300,1024]{2,0,1:T(1,128)S(1)} %copy-done, f32[300,1024]{1,0:T(8,128)S(1)} %get-tuple-element.13, f32[1,300,1024]{2,0,1:T(1,128)S(1)} %copy-done.4, f32[1,300,1024]{2,1,0:T(8,128)S(1)} %get-tuple-element.12), kind=kLoop, calls=%fused_computation.47 | loop fusion | flops 921600 | bytes 7372800 | tf_op jit(solution)/shard_map/sub | solution.py:45
  293.0 10.4 %reduce-scatter.4.cloned.1.call-done = bf16[1,300,1024]{2,1,0:T(8,128)(2,1)} async-done(((bf16[16,300,1024]{2,1,0:T(8,128)(2,1)}), bf16[1,300,1024]{2,1,0:T(8,128)(2,1)}) %reduce-scatter.4.cloned.1.call-update) | async-done | bytes 614416
  303.4 2.2 fusion.26
  305.5 2.3 copy.20
  307.8 2.3 copy.21
  (43 shorter events, 1.5 us)
Async XLA Ops:
  14.6 7.4 %copy-start = (f32[1,300,1024]{2,0,1:T(1,128)S(1)}, f32[1,300,1024]{2,0,1:T(1,128)}, u32[]{:S(2)}) copy-start(f32[1,300,1024]{2,0,1:T(1,128)} %param.8) | copy-start | bytes 3686404
  14.6 8.7 %copy-start.5 = (s32[3]{0:T(128)S(1)}, s32[3]{0:T(128)}, u32[]{:S(2)}) copy-start(s32[3]{0:T(128)} %param.13) | copy-start | bytes 40
  14.6 17.1 %copy-start.6 = (s32[3]{0:T(128)S(1)}, s32[3]{0:T(128)}, u32[]{:S(2)}) copy-start(s32[3]{0:T(128)} %param.14) | copy-start | bytes 40
  14.6 155.1 %all-to-all-start = ((bf16[16,1,300,1024]{3,2,1,0:T(8,128)(2,1)}), bf16[16,1,300,1024]{3,2,1,0:T(8,128)(2,1)}, u32[]{:S(2)}, u32[]{:S(2)}) async-start(bf16[16,1,300,1024]{3,2,1,0:T(8,128)(2,1)} %stack.2), calls=%async_computation | async-start | bytes 19922944 | tf_op jit(solution)/shard_map/all_to_all | solution.py:62
  22.0 41.2 %all-gather.2.cloned.1.call-start = ((), (), s32[]{:S(2)}) async-start(), calls=%async_computation.3 | async-start | bytes 5603328 | tf_op jit(solution)/shard_map/all_gather | solution.py:56
  23.0 280.3 %reduce-scatter.4.cloned.1.call-start = ((), (), s32[]{:S(2)}) async-start(), calls=%async_computation.4 | async-start | bytes 10584064
  169.7 21.9 %slice-start.5 = ((s8[12582912]{0:T(1024)(128)(4,1)}), s8[4194304]{0:T(1024)(128)(4,1)S(1)}, s32[]{:S(2)}) async-start(s8[12582912]{0:T(1024)(128)(4,1)} %bitcast.139), calls=%async_computation.10 | async-start | bytes 8388608
  169.7 21.9 %slice-start.6 = ((s8[12582912]{0:T(1024)(128)(4,1)}), s8[4194304]{0:T(1024)(128)(4,1)S(1)}, s32[]{:S(2)}) async-start(s8[12582912]{0:T(1024)(128)(4,1)} %bitcast.139), calls=%async_computation.11 | async-start | bytes 8388608
  177.9 9.3 %copy-start.7 = (bf16[1024,1024]{1,0:T(8,128)(2,1)S(1)}, bf16[1024,1024]{1,0:T(8,128)(2,1)}, u32[]{:S(2)}) copy-start(bf16[1024,1024]{1,0:T(8,128)(2,1)} %fusion.14) | copy-start | bytes 6291460
  177.9 13.8 %slice-start.7 = ((s8[12582912]{0:T(1024)(128)(4,1)}), s8[4194304]{0:T(1024)(128)(4,1)S(1)}, s32[]{:S(2)}) async-start(s8[12582912]{0:T(1024)(128)(4,1)} %bitcast.139), calls=%async_computation.12 | async-start | bytes 8388608
  190.1 7.2 %slice-start = ((s8[19922944]{0:T(1024)(128)(4,1)}), s8[4194304]{0:T(1024)(128)(4,1)S(1)}, s32[]{:S(2)}) async-start(s8[19922944]{0:T(1024)(128)(4,1)} %bitcast.136), calls=%async_computation.5 | async-start | bytes 8388608
  191.7 5.6 %slice-start.1 = ((s8[19922944]{0:T(1024)(128)(4,1)}), s8[4194304]{0:T(1024)(128)(4,1)S(1)}, s32[]{:S(2)}) async-start(s8[19922944]{0:T(1024)(128)(4,1)} %bitcast.136), calls=%async_computation.6 | async-start | bytes 8388608
  191.7 5.6 %slice-start.2 = ((s8[19922944]{0:T(1024)(128)(4,1)}), s8[4194304]{0:T(1024)(128)(4,1)S(1)}, s32[]{:S(2)}) async-start(s8[19922944]{0:T(1024)(128)(4,1)} %bitcast.136), calls=%async_computation.7 | async-start | bytes 8388608
  191.7 5.6 %slice-start.3 = ((s8[19922944]{0:T(1024)(128)(4,1)}), s8[4194304]{0:T(1024)(128)(4,1)S(1)}, s32[]{:S(2)}) async-start(s8[19922944]{0:T(1024)(128)(4,1)} %bitcast.136), calls=%async_computation.8 | async-start | bytes 8388608
  191.7 6.1 %slice-start.4 = ((s8[19922944]{0:T(1024)(128)(4,1)}), s8[3145728]{0:T(1024)(128)(4,1)S(1)}, s32[]{:S(2)}) async-start(s8[19922944]{0:T(1024)(128)(4,1)} %bitcast.136), calls=%async_computation.9 | async-start | bytes 6291456
  205.5 1.3 copy-start.2
  213.7 1.6 copy-start.8
  217.4 2.2 copy-start.3
  285.5 1.5 copy-start.4
  287.0 16.4 %copy-start.1 = (f32[1,300,1024]{2,0,1:T(1,128)S(1)}, f32[1,300,1024]{2,0,1:T(1,128)}, u32[]{:S(2)}) copy-start(f32[1,300,1024]{2,0,1:T(1,128)} %param.9) | copy-start | bytes 3686404
Sparse Core Ops, SparseCore 0:
  25.0 38.0 all-gather.1
  213.9 89.4 reduce-scatter.3
